TPU v7x, 32 devices: a whole 2x2x4 slice. The times are simulated.
32 devices in a mesh: row: 2 (over core), col: 4 (over z), depth: 4 (over y, x).
Axes of the slice: x: 2, y: 2, z: 4, core: 2. Of those that a mesh axis runs over, the one named last changes fastest.
Arguments:
- tokens: bfloat16 [768, 4096], P(('col', 'depth'), 'row'), may hold values from -6 to 6
- cotangent: bfloat16 [768, 4096], P(('col', 'depth'), 'row'), may hold values from -6 to 6
- gate_weight: bfloat16 [4096, 14336], P(('row', 'depth'), 'col'), may hold values from -0.09375 to 0.09375
- up_weight: bfloat16 [4096, 14336], P(('row', 'depth'), 'col'), may hold values from -0.09375 to 0.09375
- down_weight: bfloat16 [14336, 4096], P('col', ('row', 'depth')), may hold values from -0.046875 to 0.046875
Outputs:
- output: bfloat16 [768, 4096], P(('col', 'depth'), 'row')
- input_grad: bfloat16 [768, 4096], P(('col', 'depth'), 'row')
- gate_grad: float32 [4096, 14336], P(('row', 'depth'), 'col')
- up_grad: float32 [4096, 14336], P(('row', 'depth'), 'col')
- down_grad: float32 [14336, 4096], P('col', ('row', 'depth'))
All inputs are finite; a program needn't handle non-finite values.
Results may differ from a plain program's by a relative error of at most 0.0049.
Values may be sent and summed in bfloat16 or wider, within the bound.
No kernel may reach another device: no remote copies, remote signals or barrier semaphores. Data moves between devices by JAX's collectives and lax.ppermute only.
A program may use at most 192 MiB of HBM per device.

v0:
```python
import jax
import jax.numpy as jnp
from jax import lax
from jax.sharding import PartitionSpec as P


def dot_tn(left, right):
    return lax.dot_general(
        left, right, (((0,), (0,)), ((), ())), preferred_element_type=jnp.float32
    )


def dot_nt(left, right):
    return lax.dot_general(
        left, right, (((1,), (1,)), ((), ())), preferred_element_type=jnp.float32
    )


def deltas(hidden_grad, gate, up):
    sig = jax.nn.sigmoid(gate)
    gate_delta = (hidden_grad * up * sig * (1.0 + gate * (1.0 - sig))).astype(jnp.bfloat16)
    up_delta = (hidden_grad * gate * sig).astype(jnp.bfloat16)
    return (gate_delta, up_delta)


def activate(gate, up):
    return (gate * jax.nn.sigmoid(gate) * up).astype(jnp.bfloat16)


def on_device(tokens, cotangent, gate_weight, up_weight, down_weight):
    gate_full, up_full = (
        lax.all_gather(gate_weight, "depth", axis=0, tiled=True),
        lax.all_gather(up_weight, "depth", axis=0, tiled=True),
    )
    down_full = lax.all_gather(down_weight, "depth", axis=1, tiled=True)
    tok_rows, cot_rows = (
        lax.all_gather(tokens, "col", axis=0, tiled=True),
        lax.all_gather(cotangent, "col", axis=0, tiled=True),
    )
    gate = lax.psum_scatter(
        jnp.dot(tok_rows, gate_full, preferred_element_type=jnp.float32),
        "row",
        scatter_dimension=0,
        tiled=True,
    )
    up = lax.psum_scatter(
        jnp.dot(tok_rows, up_full, preferred_element_type=jnp.float32),
        "row",
        scatter_dimension=0,
        tiled=True,
    )
    hid_rows = lax.all_gather(activate(gate, up), "row", axis=0, tiled=True)
    hidden_grad = lax.psum_scatter(
        dot_nt(cot_rows, down_full), "row", scatter_dimension=0, tiled=True
    )
    gate_delta, up_delta = deltas(hidden_grad, gate, up)
    gd_rows, ud_rows = (
        lax.all_gather(gate_delta, "row", axis=0, tiled=True),
        lax.all_gather(up_delta, "row", axis=0, tiled=True),
    )
    output = lax.psum_scatter(
        jnp.dot(hid_rows, down_full, preferred_element_type=jnp.float32),
        "col",
        scatter_dimension=0,
        tiled=True,
    ).astype(jnp.bfloat16)
    input_grad = lax.psum_scatter(
        dot_nt(gd_rows, gate_full) + dot_nt(ud_rows, up_full),
        "col",
        scatter_dimension=0,
        tiled=True,
    ).astype(jnp.bfloat16)
    tok_part, cot_part = (
        lax.all_to_all(tok_rows, "depth", split_axis=1, concat_axis=0, tiled=True),
        lax.all_to_all(cot_rows, "depth", split_axis=1, concat_axis=0, tiled=True),
    )
    gd_all, ud_all, hid_all = (
        lax.all_gather(gd_rows, "depth", axis=0, tiled=True),
        lax.all_gather(ud_rows, "depth", axis=0, tiled=True),
        lax.all_gather(hid_rows, "depth", axis=0, tiled=True),
    )
    gate_grad = dot_tn(tok_part, gd_all)
    up_grad = dot_tn(tok_part, ud_all)
    down_grad = dot_tn(hid_all, cot_part)
    return (output, input_grad, gate_grad, up_grad, down_grad)


def solution(mesh):
    return jax.shard_map(
        on_device,
        mesh=mesh,
        in_specs=(
            P(("col", "depth"), "row"),
            P(("col", "depth"), "row"),
            P(("row", "depth"), "col"),
            P(("row", "depth"), "col"),
            P("col", ("row", "depth")),
        ),
        out_specs=(
            P(("col", "depth"), "row"),
            P(("col", "depth"), "row"),
            P(("row", "depth"), "col"),
            P(("row", "depth"), "col"),
            P("col", ("row", "depth")),
        ),
        check_vma=False,
    )
```

profile of v0, /device:TPU:0, one launch (start us, length us, event | category | flops | bytes accessed | tf_op | source)
XLA Modules:
  0.0 807.5 jit_solution(1116714497966719239)
XLA Ops:
  9.6 21.3 %all_gather.33 = bf16[192,2048]{1,0:T(8,128)(2,1)S(1)} all-gather(bf16[48,2048]{1,0:T(8,128)(2,1)S(1)} %copy-done), channel_id=1, replica_groups=mesh['row'=2,'col'=4,'depth'=4] {'col'}, dimensions={0}, use_global_device_ids=true | all-gather | bytes 983040 | tf_op jit(solution)/shard_map/all_gather | solution.py:37
  30.9 121.7 %all-gather.10.cloned.1.call-done = bf16[2048,3584]{1,0:T(8,128)(2,1)} async-done(((bf16[512,3584]{1,0:T(8,128)(2,1)}), bf16[2048,3584]{1,0:T(8,128)(2,1)}) %all-gather.10.cloned.1.call-update) | async-done | bytes 14680080 | tf_op jit(solution)/shard_map/all_gather | solution.py:32
  152.5 9.8 %fusion = f32[192,3584]{1,0:T(8,128)} fusion(bf16[192,2048]{1,0:T(8,128)(2,1)S(1)} %all_gather.33, bf16[2048,3584]{1,0:T(8,128)(2,1)} %all-gather.10.cloned.1.call-done), kind=kOutput, calls=%fused_computation.9 | convolution fusion | flops 2818572288 | bytes 18219008 | tf_op jit(solution)/shard_map/dot_general | solution.py:41
  162.4 132.0 %all-gather.12.cloned.1.call-done = bf16[2048,3584]{1,0:T(8,128)(2,1)} async-done(((bf16[512,3584]{1,0:T(8,128)(2,1)}), bf16[2048,3584]{1,0:T(8,128)(2,1)}) %all-gather.12.cloned.1.call-update) | async-done | bytes 14680080 | tf_op jit(solution)/shard_map/all_gather | solution.py:33
  294.4 9.8 %fusion.1 = f32[192,3584]{1,0:T(8,128)} fusion(bf16[192,2048]{1,0:T(8,128)(2,1)S(1)} %all_gather.33, bf16[2048,3584]{1,0:T(8,128)(2,1)} %all-gather.12.cloned.1.call-done), kind=kOutput, calls=%fused_computation.10 | convolution fusion | flops 2818572288 | bytes 18219008 | tf_op jit(solution)/shard_map/dot_general | solution.py:47
  305.2 19.5 %all_gather.38 = bf16[192,2048]{1,0:T(8,128)(2,1)S(1)} all-gather(bf16[48,2048]{1,0:T(8,128)(2,1)S(1)} %copy-done.1), channel_id=1, replica_groups=mesh['row'=2,'col'=4,'depth'=4] {'col'}, dimensions={0}, use_global_device_ids=true | all-gather | bytes 983040 | tf_op jit(solution)/shard_map/all_gather | solution.py:38
  324.7 111.3 %all-gather.16.cloned.1.call-done = bf16[3584,2048]{1,0:T(8,128)(2,1)} async-done(((bf16[3584,512]{1,0:T(8,128)(2,1)}), bf16[3584,2048]{1,0:T(8,128)(2,1)}) %all-gather.16.cloned.1.call-update) | async-done | bytes 14680080 | tf_op jit(solution)/shard_map/all_gather | solution.py:35
  436.1 11.7 %fusion.3 = f32[192,3584]{1,0:T(8,128)} fusion(bf16[192,2048]{1,0:T(8,128)(2,1)S(1)} %all_gather.38, bf16[3584,2048]{1,0:T(8,128)(2,1)} %all-gather.16.cloned.1.call-done), kind=kOutput, calls=%fused_computation.12 | convolution fusion | flops 2818572288 | bytes 18219008 | tf_op jit(solution)/shard_map/dot_general | solution.py:14
  449.1 14.3 %reduce-scatter.8.cloned.1.call-done = f32[96,3584]{1,0:T(8,128)} async-done(((f32[192,3584]{1,0:T(8,128)}), f32[96,3584]{1,0:T(8,128)}) %reduce-scatter.8.cloned.1.call-update) | async-done | bytes 1376272 | tf_op jit(solution)/shard_map/reduce_scatter | solution.py:46
  463.5 14.3 %reduce-scatter.12.cloned.1.call-done = f32[96,3584]{1,0:T(8,128)} async-done(((f32[192,3584]{1,0:T(8,128)}), f32[96,3584]{1,0:T(8,128)}) %reduce-scatter.12.cloned.1.call-update) | async-done | bytes 1376272 | tf_op jit(solution)/shard_map/reduce_scatter | solution.py:53
  483.7 9.2 %all-gather.18.cloned.1.call-done = bf16[192,3584]{1,0:T(8,128)(2,1)} async-done(((bf16[96,3584]{1,0:T(8,128)(2,1)}), bf16[192,3584]{1,0:T(8,128)(2,1)}) %all-gather.18.cloned.1.call-update) | async-done | bytes 1376272 | tf_op jit(solution)/shard_map/all_gather | solution.py:58
  492.9 8.5 %fusion.4 = f32[192,2048]{1,0:T(8,128)S(1)} fusion(bf16[192,3584]{1,0:T(8,128)(2,1)} %all-gather.18.cloned.1.call-done, bf16[2048,3584]{1,0:T(8,128)(2,1)} %all-gather.10.cloned.1.call-done), kind=kOutput, calls=%fused_computation.13 | convolution fusion | flops 2818572288 | bytes 17629184 | tf_op jit(solution)/shard_map/dot_general | solution.py:14
  505.9 11.6 %convolution_add_fusion = f32[192,2048]{1,0:T(8,128)} fusion(f32[192,2048]{1,0:T(8,128)S(1)} %fusion.4, bf16[192,3584]{1,0:T(8,128)(2,1)} %all-gather.20.cloned.1.call-done, bf16[2048,3584]{1,0:T(8,128)(2,1)} %all-gather.12.cloned.1.call-done), kind=kOutput, calls=%fused_computation.2 | convolution fusion | flops 2818965504 | bytes 19202048 | tf_op jit(solution)/shard_map/dot_general | solution.py:14
  518.8 9.8 %fusion.2 = f32[192,2048]{1,0:T(8,128)} fusion(bf16[192,3584]{1,0:T(8,128)(2,1)} %all-gather.14.cloned.1.call-done, bf16[3584,2048]{1,0:T(8,128)(2,1)} %all-gather.16.cloned.1.call-done), kind=kOutput, calls=%fused_computation.11 | convolution fusion | flops 2818572288 | bytes 17629184 | tf_op jit(solution)/shard_map/dot_general | solution.py:62
  536.3 21.8 %reduce-scatter.14.cloned.1.call-done = f32[48,2048]{1,0:T(8,128)} async-done(((f32[192,2048]{1,0:T(8,128)}), f32[48,2048]{1,0:T(8,128)}) %reduce-scatter.14.cloned.1.call-update) | async-done | bytes 393232 | tf_op jit(solution)/shard_map/reduce_scatter | solution.py:67
  559.8 35.6 %reduce-scatter.10.cloned.1.call-done = f32[48,2048]{1,0:T(8,128)} async-done(((f32[192,2048]{1,0:T(8,128)}), f32[48,2048]{1,0:T(8,128)}) %reduce-scatter.10.cloned.1.call-update) | async-done | bytes 393232 | tf_op jit(solution)/shard_map/reduce_scatter | solution.py:61
  600.8 61.3 %all-gather.22.cloned.1.call-done = bf16[768,3584]{1,0:T(8,128)(2,1)} async-done(((bf16[192,3584]{1,0:T(8,128)(2,1)}), bf16[768,3584]{1,0:T(8,128)(2,1)}) %all-gather.22.cloned.1.call-update) | async-done | bytes 5505040 | tf_op jit(solution)/shard_map/all_gather | solution.py:78
  662.1 7.7 convolution_bitcast_fusion.1
  669.8 8.8 %copy.20 = f32[512,3584]{1,0:T(8,128)} copy(f32[512,3584]{0,1:T(8,128)} %convolution_bitcast_fusion.1) | data formatting | bytes 14680064
  678.6 49.2 %all-gather.24.cloned.1.call-done = bf16[768,3584]{1,0:T(8,128)(2,1)} async-done(((bf16[192,3584]{1,0:T(8,128)(2,1)}), bf16[768,3584]{1,0:T(8,128)(2,1)}) %all-gather.24.cloned.1.call-update) | async-done | bytes 5505040 | tf_op jit(solution)/shard_map/all_gather | solution.py:79
  727.8 7.7 convolution_bitcast_fusion
  735.4 8.7 %copy.21 = f32[512,3584]{1,0:T(8,128)} copy(f32[512,3584]{0,1:T(8,128)} %convolution_bitcast_fusion) | data formatting | bytes 14680064
  744.2 49.1 %all-gather.26.cloned.1.call-done = bf16[768,3584]{1,0:T(8,128)(2,1)} async-done(((bf16[192,3584]{1,0:T(8,128)(2,1)}), bf16[768,3584]{1,0:T(8,128)(2,1)}) %all-gather.26.cloned.1.call-update) | async-done | bytes 5505040 | tf_op jit(solution)/shard_map/all_gather | solution.py:80
  793.2 7.7 fusion.5
  (44 shorter events, 31.2 us)
Async XLA Ops:
  7.2 145.4 %all-gather.10.cloned.1.call-start = ((), (), s32[]{:S(2)}) async-start(), calls=%async_computation.7 | async-start | bytes 18350080 | tf_op jit(solution)/shard_map/all_gather | solution.py:32
  7.9 286.5 %all-gather.12.cloned.1.call-start = ((), (), s32[]{:S(2)}) async-start(), calls=%async_computation.9 | async-start | bytes 18350080 | tf_op jit(solution)/shard_map/all_gather | solution.py:33
  8.6 0.9 copy-start
  8.7 427.4 %all-gather.16.cloned.1.call-start = ((), (), s32[]{:S(2)}) async-start(), calls=%async_computation.12 | async-start | bytes 18350080 | tf_op jit(solution)/shard_map/all_gather | solution.py:35
  9.4 439.7 %reduce-scatter.6.cloned.1.call-start = ((), (), s32[]{:S(2)}) async-start(), calls=%async_computation.8 | async-start | bytes 4128768 | tf_op jit(solution)/shard_map/reduce_scatter | solution.py:40
  162.4 301.1 %reduce-scatter.8.cloned.1.call-start = ((), (), s32[]{:S(2)}) async-start(), calls=%async_computation.10 | async-start | bytes 4128768 | tf_op jit(solution)/shard_map/reduce_scatter | solution.py:46
  304.2 1.0 copy-start.1
  304.2 173.5 %reduce-scatter.12.cloned.1.call-start = ((), (), s32[]{:S(2)}) async-start(), calls=%async_computation.14 | async-start | bytes 4128768 | tf_op jit(solution)/shard_map/reduce_scatter | solution.py:53
  447.8 45.2 %all-gather.18.cloned.1.call-start = ((), (), s32[]{:S(2)}) async-start(), calls=%async_computation.15 | async-start | bytes 2064384 | tf_op jit(solution)/shard_map/all_gather | solution.py:58
  482.0 23.9 %all-gather.20.cloned.1.call-start = ((), (), s32[]{:S(2)}) async-start(), calls=%async_computation.16 | async-start | bytes 2064384 | tf_op jit(solution)/shard_map/all_gather | solution.py:59
  482.8 36.1 %all-gather.14.cloned.1.call-start = ((), (), s32[]{:S(2)}) async-start(), calls=%async_computation.11 | async-start | bytes 2064384 | tf_op jit(solution)/shard_map/all_gather | solution.py:52
  483.5 74.6 %reduce-scatter.14.cloned.1.call-start = ((), (), s32[]{:S(2)}) async-start(), calls=%async_computation.17 | async-start | bytes 1966080 | tf_op jit(solution)/shard_map/reduce_scatter | solution.py:67
  517.6 77.9 %reduce-scatter.10.cloned.1.call-start = ((), (), s32[]{:S(2)}) async-start(), calls=%async_computation.13 | async-start | bytes 1966080 | tf_op jit(solution)/shard_map/reduce_scatter | solution.py:61
  528.6 133.5 %all-gather.22.cloned.1.call-start = ((), (), s32[]{:S(2)}) async-start(), calls=%async_computation.18 | async-start | bytes 6881280 | tf_op jit(solution)/shard_map/all_gather | solution.py:78
  529.2 198.6 %all-gather.24.cloned.1.call-start = ((), (), s32[]{:S(2)}) async-start(), calls=%async_computation.19 | async-start | bytes 6881280 | tf_op jit(solution)/shard_map/all_gather | solution.py:79
  529.9 263.3 %all-gather.26.cloned.1.call-start = ((), (), s32[]{:S(2)}) async-start(), calls=%async_computation.20 | async-start | bytes 6881280 | tf_op jit(solution)/shard_map/all_gather | solution.py:80
  531.5 65.6 %all-to-all-start = ((bf16[192,4,512]{2,0,1:T(8,128)(2,1)}), bf16[192,4,512]{2,0,1:T(8,128)(2,1)S(1)}, u32[]{:S(2)}, u32[]{:S(2)}) async-start(bf16[192,4,512]{2,0,1:T(8,128)(2,1)} %bitcast.35), calls=%async_computation.5 | async-start | bytes 1572864 | tf_op jit(solution)/shard_map/all_to_all | solution.py:74
  597.1 147.1 %all-to-all-start.1 = ((bf16[192,4,512]{2,0,1:T(8,128)(2,1)}), bf16[192,4,512]{2,0,1:T(8,128)(2,1)S(1)}, u32[]{:S(2)}, u32[]{:S(2)}) async-start(bf16[192,4,512]{2,0,1:T(8,128)(2,1)} %bitcast.34), calls=%async_computation.6 | async-start | bytes 1572864 | tf_op jit(solution)/shard_map/all_to_all | solution.py:75
Sparse Core Ops, SparseCore 0:
  9.8 142.6 all-gather.9
  154.4 139.9 all-gather.11
  296.2 139.8 all-gather.15
  438.8 10.3 reduce-scatter.5
  451.9 11.5 reduce-scatter.7
  466.1 11.5 reduce-scatter.11
  482.1 10.7 all-gather.17
  495.1 10.7 all-gather.19
  508.1 10.6 all-gather.13
  521.7 36.4 reduce-scatter.13
  561.1 34.2 reduce-scatter.9
  597.3 64.8 all-gather.21
  664.1 63.6 all-gather.23
  729.6 63.6 all-gather.25
where the time goes:
time: 808 us; the launch traced here: 807 us
  waiting for transfers between devices  632 us (78%)
  matrix products  84.2 us (10%)
  blocking collectives  40.8 us (5%)
  local copies, waits for them, and re-layouts  20.5 us (3%)
  between operations  14 us (2%)
  starting transfers between devices  8.36 us (1%)
    all_gather x1, waiting for transfers between devices, on_device(): lax.all_gather(up_weight, 'depth', axis=0, tiled=True)  132 us
    all_gather x1, waiting for transfers between devices, on_device(): lax.all_gather(gate_weight, 'depth', axis=0, tiled=True)  122 us
    all_gather x1, waiting for transfers between devices, on_device(): down_full = lax.all_gather(down_weight, 'depth', axis=1, tiled=True)  111 us
    all_gather x1, waiting for transfers between devices, on_device(): lax.all_gather(gd_rows, 'depth', axis=0, tiled=True)  61.3 us
    all_gather x1, waiting for transfers between devices, on_device(): lax.all_gather(ud_rows, 'depth', axis=0, tiled=True)  49.2 us
    all_gather x1, waiting for transfers between devices, on_device(): lax.all_gather(hid_rows, 'depth', axis=0, tiled=True)  49.1 us
    reduce_scatter x1, waiting for transfers between devices, on_device(): lax.psum_scatter(jnp.dot(hid_rows, down_full, preferred_element_type=jnp....  35.6 us
    dot_general x3, matrix products, dot_nt(): lax.dot_general(left, right, (((1,), (1,)), ((), ())), preferred_element_...  31.8 us
  transfers between devices with their start and end apart: 16, of which 14 were waited for; matrix products, arithmetic and copies ran while one was open for 12% of the time, Pallas kernels for 0%

commit v1 on v0

--- a/solution.py
+++ b/solution.py
@@ -32,7 +32,14 @@
         lax.all_gather(gate_weight, "depth", axis=0, tiled=True),
         lax.all_gather(up_weight, "depth", axis=0, tiled=True),
     )
-    down_full = lax.all_gather(down_weight, "depth", axis=1, tiled=True)
+    ring = [down_weight]
+    for hop in range(3):
+        ring.append(lax.ppermute(ring[-1], "depth", [(dev, (dev + 1) % 4) for dev in range(4)]))
+    down_full = jnp.roll(
+        jnp.concatenate(ring[::-1], axis=1),
+        (lax.axis_index("depth") + 1) * ring[0].shape[1],
+        axis=1,
+    )
     tok_rows, cot_rows = (
         lax.all_gather(tokens, "col", axis=0, tiled=True),
         lax.all_gather(cotangent, "col", axis=0, tiled=True),

time: 808 us -> 809 us (level)
  waiting for transfers between devices: 632 us -> 602 us
  local copies, waits for them, and re-layouts: 20.5 us -> 46.3 us
    ppermute x0 -> x3, waiting for transfers between devices: none -> 412 us  [on_device(): lax.ppermute(ring[-1], 'depth', [(dev, (dev + 1) % 4) for dev in range(4)])]
    all_gather x1, waiting for transfers between devices: 132 us -> 0.02 us  [on_device(): lax.all_gather(up_weight, 'depth', axis=0, tiled=True)]
    all_gather x1, waiting for transfers between devices: 122 us -> 0.01 us  [on_device(): lax.all_gather(gate_weight, 'depth', axis=0, tiled=True)]
    all_gather x1 -> x0, waiting for transfers between devices: 111 us -> none  [on_device(): down_full = lax.all_gather(down_weight, 'depth', axis=1, tiled=True)]
    all_gather x1, waiting for transfers between devices: 61.3 us -> 0.36 us  [on_device(): lax.all_gather(gd_rows, 'depth', axis=0, tiled=True)]
    unnamed x6 -> x19, local copies, waits for them, and re-layouts: 18.6 us -> 42.3 us
    reduce_scatter x1, waiting for transfers between devices: 35.6 us -> 20 us  [on_device(): lax.psum_scatter(jnp.dot(hid_rows, down_full, preferred_element_type=jnp....]
    reduce_scatter x1, waiting for transfers between devices: 14.3 us -> 0.02 us  [on_device(): lax.psum_scatter(dot_nt(cot_rows, down_full), 'row', scatter_dimension=0,...]
  transfers between devices with their start and end apart: 16 -> 18, of which waited for: 14 -> 13; matrix products, arithmetic and copies ran while one was open for 12% -> 15% of each run, Pallas kernels for 0% -> 0%
where the time goes in v1:
time: 809 us; the launch traced here: 808 us
  waiting for transfers between devices  602 us (74%)
  matrix products  84.1 us (10%)
  local copies, waits for them, and re-layouts  46.3 us (6%)
  blocking collectives  36.3 us (4%)
  starting transfers between devices  16.3 us (2%)
  between operations  15.4 us (2%)
    ppermute x3, waiting for transfers between devices, on_device(): lax.ppermute(ring[-1], 'depth', [(dev, (dev + 1) % 4) for dev in range(4)])  412 us
    all_gather x1, waiting for transfers between devices, on_device(): lax.all_gather(ud_rows, 'depth', axis=0, tiled=True)  49.1 us
    all_gather x1, waiting for transfers between devices, on_device(): lax.all_gather(hid_rows, 'depth', axis=0, tiled=True)  49.1 us
    unnamed x19, local copies, waits for them, and re-layouts  42.3 us
    reduce_scatter x1, waiting for transfers between devices, on_device(): lax.psum_scatter(dot_nt(gd_rows, gate_full) + dot_nt(ud_rows, up_full), '...  35.4 us
    dot_general x3, matrix products, dot_nt(): lax.dot_general(left, right, (((1,), (1,)), ((), ())), preferred_element_...  31.9 us
    dot_general x3, matrix products, dot_tn(): lax.dot_general(left, right, (((0,), (0,)), ((), ())), preferred_element_...  23.1 us
    reduce_scatter x1, waiting for transfers between devices, on_device(): lax.psum_scatter(jnp.dot(hid_rows, down_full, preferred_element_type=jnp....  20 us
  transfers between devices with their start and end apart: 18, of which 13 were waited for; matrix products, arithmetic and copies ran while one was open for 15% of the time, Pallas kernels for 0%

profile of v1, /device:TPU:0, one launch (start us, length us, event | category | flops | bytes accessed | tf_op | source)
XLA Modules:
  0.0 808.4 jit_solution(16867777893779885418)
XLA Ops:
  12.5 138.5 %collective-permute-done = bf16[3584,512]{1,0:T(8,128)(2,1)S(1)} collective-permute-done((bf16[3584,512]{1,0:T(8,128)(2,1)}, bf16[3584,512]{1,0:T(8,128)(2,1)S(1)}, u32[]{:S(2)}, u32[]{:S(2)}) %collective-permute-start) | collective-permute-done | bytes 3670048 | tf_op jit(solution)/shard_map/ppermute | solution.py:37
  155.2 141.4 %collective-permute-done.1 = bf16[3584,512]{1,0:T(8,128)(2,1)} collective-permute-done((bf16[3584,512]{1,0:T(8,128)(2,1)S(1)}, bf16[3584,512]{1,0:T(8,128)(2,1)}, u32[]{:S(2)}, u32[]{:S(2)}) %collective-permute-start.1) | collective-permute-done | bytes 3670048 | tf_op jit(solution)/shard_map/ppermute | solution.py:37
  299.3 17.8 %all_gather.34 = bf16[192,2048]{1,0:T(8,128)(2,1)S(1)} all-gather(bf16[48,2048]{1,0:T(8,128)(2,1)S(1)} %copy-done.3), channel_id=1, replica_groups=mesh['row'=2,'col'=4,'depth'=4] {'col'}, dimensions={0}, use_global_device_ids=true | all-gather | bytes 983040 | tf_op jit(solution)/shard_map/all_gather | solution.py:45
  317.1 131.7 %collective-permute-done.2 = bf16[3584,512]{1,0:T(8,128)(2,1)} collective-permute-done((bf16[3584,512]{1,0:T(8,128)(2,1)}, bf16[3584,512]{1,0:T(8,128)(2,1)}, u32[]{:S(2)}, u32[]{:S(2)}) %collective-permute-start.2) | collective-permute-done | bytes 3670048 | tf_op jit(solution)/shard_map/ppermute | solution.py:37
  452.9 4.3 constant_dynamic-update-slice_fusion.6
  473.8 11.7 %fusion.4 = f32[192,3584]{1,0:T(8,128)} fusion(bf16[192,2048]{1,0:T(8,128)(2,1)S(1)} %all_gather.34, bf16[3584,4096]{1,0:T(8,128)(2,1)} %constant_dynamic-update-slice_fusion, s32[]{:T(128)S(6)} %select_n.14), kind=kOutput, calls=%fused_computation.6 | convolution fusion | flops 2818572288 | bytes 18219012 | tf_op jit(solution)/shard_map/dot_general | solution.py:14
  485.6 18.5 %all_gather.30 = bf16[192,2048]{1,0:T(8,128)(2,1)S(1)} all-gather(bf16[48,2048]{1,0:T(8,128)(2,1)S(1)} %copy-done.4), channel_id=1, replica_groups=mesh['row'=2,'col'=4,'depth'=4] {'col'}, dimensions={0}, use_global_device_ids=true | all-gather | bytes 983040 | tf_op jit(solution)/shard_map/all_gather | solution.py:44
  504.1 9.7 %fusion.9 = f32[192,3584]{1,0:T(8,128)} fusion(bf16[192,2048]{1,0:T(8,128)(2,1)S(1)} %all_gather.30, bf16[2048,3584]{1,0:T(8,128)(2,1)} %all-gather.9.cloned.1.call-done), kind=kOutput, calls=%fused_computation.24 | convolution fusion | flops 2818572288 | bytes 18219008 | tf_op jit(solution)/shard_map/dot_general | solution.py:48
  513.9 9.7 %fusion.10 = f32[192,3584]{1,0:T(8,128)} fusion(bf16[192,2048]{1,0:T(8,128)(2,1)S(1)} %all_gather.30, bf16[2048,3584]{1,0:T(8,128)(2,1)} %all-gather.11.cloned.1.call-done), kind=kOutput, calls=%fused_computation.25 | convolution fusion | flops 2818572288 | bytes 18219008 | tf_op jit(solution)/shard_map/dot_general | solution.py:54
  525.5 14.2 %reduce-scatter.8.cloned.1.call-done = f32[96,3584]{1,0:T(8,128)} async-done(((f32[192,3584]{1,0:T(8,128)}), f32[96,3584]{1,0:T(8,128)}) %reduce-scatter.8.cloned.1.call-update) | async-done | bytes 1376272 | tf_op jit(solution)/shard_map/reduce_scatter | solution.py:53
  545.7 9.0 %all-gather.13.cloned.1.call-done = bf16[192,3584]{1,0:T(8,128)(2,1)} async-done(((bf16[96,3584]{1,0:T(8,128)(2,1)}), bf16[192,3584]{1,0:T(8,128)(2,1)}) %all-gather.13.cloned.1.call-update) | async-done | bytes 1376272 | tf_op jit(solution)/shard_map/all_gather | solution.py:59
  554.8 9.8 %fusion.2 = f32[192,2048]{1,0:T(8,128)} fusion(bf16[192,3584]{1,0:T(8,128)(2,1)} %all-gather.13.cloned.1.call-done, bf16[3584,4096]{1,0:T(8,128)(2,1)} %constant_dynamic-update-slice_fusion, s32[]{:T(128)S(6)} %select_n.14), kind=kOutput, calls=%fused_computation.2 | convolution fusion | flops 2818572288 | bytes 17629188 | tf_op jit(solution)/shard_map/dot_general | solution.py:69
  567.6 8.5 %fusion.11 = f32[192,2048]{1,0:T(8,128)S(1)} fusion(bf16[192,3584]{1,0:T(8,128)(2,1)} %all-gather.15.cloned.1.call-done, bf16[2048,3584]{1,0:T(8,128)(2,1)} %all-gather.9.cloned.1.call-done), kind=kOutput, calls=%fused_computation.26 | convolution fusion | flops 2818572288 | bytes 17629184 | tf_op jit(solution)/shard_map/dot_general | solution.py:14
  576.2 4.3 all-gather.17.cloned.1.call-done
  580.5 11.6 %convolution_add_fusion = f32[192,2048]{1,0:T(8,128)} fusion(f32[192,2048]{1,0:T(8,128)S(1)} %fusion.11, bf16[192,3584]{1,0:T(8,128)(2,1)} %all-gather.17.cloned.1.call-done, bf16[2048,3584]{1,0:T(8,128)(2,1)} %all-gather.11.cloned.1.call-done), kind=kOutput, calls=%fused_computation.7 | convolution fusion | flops 2818965504 | bytes 19202048 | tf_op jit(solution)/shard_map/dot_general | solution.py:14
  599.9 20.0 %reduce-scatter.10.cloned.1.call-done = f32[48,2048]{1,0:T(8,128)} async-done(((f32[192,2048]{1,0:T(8,128)}), f32[48,2048]{1,0:T(8,128)}) %reduce-scatter.10.cloned.1.call-update) | async-done | bytes 393232 | tf_op jit(solution)/shard_map/reduce_scatter | solution.py:68
  621.5 35.4 %reduce-scatter.14.cloned.1.call-done = f32[48,2048]{1,0:T(8,128)} async-done(((f32[192,2048]{1,0:T(8,128)}), f32[48,2048]{1,0:T(8,128)}) %reduce-scatter.14.cloned.1.call-update) | async-done | bytes 393232 | tf_op jit(solution)/shard_map/reduce_scatter | solution.py:74
  662.7 7.7 convolution_bitcast_fusion.1
  670.4 8.7 %copy.20 = f32[512,3584]{1,0:T(8,128)} copy(f32[512,3584]{0,1:T(8,128)} %convolution_bitcast_fusion.1) | data formatting | bytes 14680064
  679.1 49.1 %all-gather.21.cloned.1.call-done = bf16[768,3584]{1,0:T(8,128)(2,1)} async-done(((bf16[192,3584]{1,0:T(8,128)(2,1)}), bf16[768,3584]{1,0:T(8,128)(2,1)}) %all-gather.21.cloned.1.call-update) | async-done | bytes 5505040 | tf_op jit(solution)/shard_map/all_gather | solution.py:86
  728.2 7.7 convolution_bitcast_fusion
  735.9 8.7 %copy.21 = f32[512,3584]{1,0:T(8,128)} copy(f32[512,3584]{0,1:T(8,128)} %convolution_bitcast_fusion) | data formatting | bytes 14680064
  744.6 49.1 %all-gather.23.cloned.1.call-done = bf16[768,3584]{1,0:T(8,128)(2,1)} async-done(((bf16[192,3584]{1,0:T(8,128)(2,1)}), bf16[768,3584]{1,0:T(8,128)(2,1)}) %all-gather.23.cloned.1.call-update) | async-done | bytes 5505040 | tf_op jit(solution)/shard_map/all_gather | solution.py:87
  793.6 7.7 fusion.12
  (61 shorter events, 58.2 us)
Async XLA Ops:
  8.0 291.3 %copy-start.3 = (bf16[48,2048]{1,0:T(8,128)(2,1)S(1)}, bf16[48,2048]{1,0:T(8,128)(2,1)}, u32[]{:S(2)}) copy-start(bf16[48,2048]{1,0:T(8,128)(2,1)} %param.6) | copy-start | bytes 589828
  8.0 496.1 %all-gather.9.cloned.1.call-start = ((), (), s32[]{:S(2)}) async-start(), calls=%async_computation.7 | async-start | bytes 18350080 | tf_op jit(solution)/shard_map/all_gather | solution.py:32
  8.7 505.2 %all-gather.11.cloned.1.call-start = ((), (), s32[]{:S(2)}) async-start(), calls=%async_computation.9 | async-start | bytes 18350080 | tf_op jit(solution)/shard_map/all_gather | solution.py:33
  9.5 514.3 %reduce-scatter.12.cloned.1.call-start = ((), (), s32[]{:S(2)}) async-start(), calls=%async_computation.13 | async-start | bytes 4128768 | tf_op jit(solution)/shard_map/reduce_scatter | solution.py:60
  9.5 141.5 %collective-permute-start = (bf16[3584,512]{1,0:T(8,128)(2,1)}, bf16[3584,512]{1,0:T(8,128)(2,1)S(1)}, u32[]{:S(2)}, u32[]{:S(2)}) collective-permute-start(bf16[3584,512]{1,0:T(8,128)(2,1)} %param.9), channel_id=1, source_target_pairs={{0,1},{1,2},{2,3},{3,0},{4,5},{5,6},{6,7},{7,4},{8,9},{9,10},{10,1... | collective-permute-start | bytes 11010056 | tf_op jit(solution)/shard_map/ppermute | solution.py:37
  151.0 1.8 copy-start.1
  152.8 143.8 %collective-permute-start.1 = (bf16[3584,512]{1,0:T(8,128)(2,1)S(1)}, bf16[3584,512]{1,0:T(8,128)(2,1)}, u32[]{:S(2)}, u32[]{:S(2)}) collective-permute-start(bf16[3584,512]{1,0:T(8,128)(2,1)S(1)} %collective-permute-done), channel_id=1, source_target_pairs={{0,1},{1,2},{2,3},{3,0},{4,5},{5,6},{6,7},{7,4},{8,9},{9,10},{10,1... | collective-permute-start | bytes 11010056 | tf_op jit(solution)/shard_map/ppermute | solution.py:37
  296.7 152.1 %collective-permute-start.2 = (bf16[3584,512]{1,0:T(8,128)(2,1)}, bf16[3584,512]{1,0:T(8,128)(2,1)}, u32[]{:S(2)}, u32[]{:S(2)}) collective-permute-start(bf16[3584,512]{1,0:T(8,128)(2,1)} %collective-permute-done.1), channel_id=1, source_target_pairs={{0,1},{1,2},{2,3},{3,0},{4,5},{5,6},{6,7},{7,4},{8,9},{9,10},{10,1... | collective-permute-start | bytes 11010056 | tf_op jit(solution)/shard_map/ppermute | solution.py:37
  452.9 4.3 copy-start.2
  452.9 6.4 copy-start
  473.8 11.8 %copy-start.4 = (bf16[48,2048]{1,0:T(8,128)(2,1)S(1)}, bf16[48,2048]{1,0:T(8,128)(2,1)}, u32[]{:S(2)}) copy-start(bf16[48,2048]{1,0:T(8,128)(2,1)} %param.5) | copy-start | bytes 589828
  485.6 40.0 %reduce-scatter.6.cloned.1.call-start = ((), (), s32[]{:S(2)}) async-start(), calls=%async_computation.8 | async-start | bytes 4128768 | tf_op jit(solution)/shard_map/reduce_scatter | solution.py:47
  513.8 25.9 %reduce-scatter.8.cloned.1.call-start = ((), (), s32[]{:S(2)}) async-start(), calls=%async_computation.10 | async-start | bytes 4128768 | tf_op jit(solution)/shard_map/reduce_scatter | solution.py:53
  523.7 31.1 %all-gather.13.cloned.1.call-start = ((), (), s32[]{:S(2)}) async-start(), calls=%async_computation.11 | async-start | bytes 2064384 | tf_op jit(solution)/shard_map/all_gather | solution.py:59
  544.0 23.6 %all-gather.15.cloned.1.call-start = ((), (), s32[]{:S(2)}) async-start(), calls=%async_computation.14 | async-start | bytes 2064384 | tf_op jit(solution)/shard_map/all_gather | solution.py:65
  544.8 35.7 %all-gather.17.cloned.1.call-start = ((), (), s32[]{:S(2)}) async-start(), calls=%async_computation.15 | async-start | bytes 2064384 | tf_op jit(solution)/shard_map/all_gather | solution.py:66
  545.5 74.3 %reduce-scatter.10.cloned.1.call-start = ((), (), s32[]{:S(2)}) async-start(), calls=%async_computation.12 | async-start | bytes 1966080 | tf_op jit(solution)/shard_map/reduce_scatter | solution.py:68
  564.5 92.4 %reduce-scatter.14.cloned.1.call-start = ((), (), s32[]{:S(2)}) async-start(), calls=%async_computation.16 | async-start | bytes 1966080 | tf_op jit(solution)/shard_map/reduce_scatter | solution.py:74
  592.1 70.5 %all-gather.19.cloned.1.call-start = ((), (), s32[]{:S(2)}) async-start(), calls=%async_computation.17 | async-start | bytes 6881280 | tf_op jit(solution)/shard_map/all_gather | solution.py:85
  592.9 135.3 %all-gather.21.cloned.1.call-start = ((), (), s32[]{:S(2)}) async-start(), calls=%async_computation.18 | async-start | bytes 6881280 | tf_op jit(solution)/shard_map/all_gather | solution.py:86
  593.4 200.2 %all-gather.23.cloned.1.call-start = ((), (), s32[]{:S(2)}) async-start(), calls=%async_computation.19 | async-start | bytes 6881280 | tf_op jit(solution)/shard_map/all_gather | solution.py:87
  595.0 63.6 %all-to-all-start = ((bf16[192,4,512]{2,0,1:T(8,128)(2,1)}), bf16[192,4,512]{2,0,1:T(8,128)(2,1)S(1)}, u32[]{:S(2)}, u32[]{:S(2)}) async-start(bf16[192,4,512]{2,0,1:T(8,128)(2,1)} %bitcast.35), calls=%async_computation.5 | async-start | bytes 1572864 | tf_op jit(solution)/shard_map/all_to_all | solution.py:81
  658.6 86.0 %all-to-all-start.1 = ((bf16[192,4,512]{2,0,1:T(8,128)(2,1)}), bf16[192,4,512]{2,0,1:T(8,128)(2,1)S(1)}, u32[]{:S(2)}, u32[]{:S(2)}) async-start(bf16[192,4,512]{2,0,1:T(8,128)(2,1)} %bitcast.34), calls=%async_computation.6 | async-start | bytes 1572864 | tf_op jit(solution)/shard_map/all_to_all | solution.py:82
Sparse Core Ops, SparseCore 0:
  10.8 256.4 all-gather.8
  269.1 217.6 all-gather.10
  595.0 67.6 all-gather.18
  664.5 63.6 all-gather.20
  730.0 63.6 all-gather.22
Sparse Core Ops, SparseCore 1:
  485.7 12.2 reduce-scatter.11
  513.9 11.5 reduce-scatter.5
  528.2 11.5 reduce-scatter.7
  544.1 10.6 all-gather.12
  557.0 10.6 all-gather.14
  569.8 10.6 all-gather.16
  583.3 36.5 reduce-scatter.9
  622.7 34.1 reduce-scatter.13
